TPU v7x, 512 devices: a whole 4x4x16 slice. The times are simulated.
512 devices in a mesh: seq: 32 (over x, y, core), head: 16 (over z).
Axes of the slice: x: 4, y: 4, z: 16, core: 2. Of those that a mesh axis runs over, the one named last changes fastest.
Arguments:
- queries: bfloat16 [32768, 4096], P('seq', 'head'), may hold values from -6 to 6
- keys: bfloat16 [32768, 4096], P('seq', 'head'), may hold values from -6 to 6
- values: bfloat16 [32768, 4096], P('seq', 'head'), may hold values from -6 to 6
- out_weight: bfloat16 [4096, 4096], P(None, 'head'), may hold values from -0.09375 to 0.09375
Outputs:
- output: bfloat16 [32768, 4096], P('seq', 'head')
All inputs are finite; a program needn't handle non-finite values.
Results may differ from a plain program's by a relative error of at most 0.0058.
Values may be sent and summed in bfloat16 or wider, within the bound.
A program may use at most 64 MiB of HBM per device.

v0:
```python
import jax
import jax.numpy as jnp
from jax import lax
from jax.sharding import PartitionSpec as P

HD = 128
BLOCK = 1024


def prefix_2(value, axis, join, neutral):
    count, mine = (lax.axis_size(axis), lax.axis_index(axis))
    pieces = lax.all_gather(value, axis)
    running = jnp.full_like(value, 0) + jnp.asarray(neutral, value.dtype)

    def step(position, running):
        longer = join(running, pieces[position])
        return jnp.where(position < mine, longer, running)

    return lax.fori_loop(0, count - 1, step, running)


def add_states(earlier, later):
    return earlier + later


def per_device(queries, keys, values, out_weight):
    tok_rows = queries.shape[0]
    local_heads = queries.shape[1] // HD
    blocks_count = tok_rows // BLOCK
    block_shape = (blocks_count, BLOCK, local_heads, HD)
    query_blocks = queries.reshape(block_shape)
    key_blocks = keys.reshape(block_shape)
    value_blocks = values.reshape(block_shape)
    block_states = jnp.einsum(
        "cthd,cthe->chde", key_blocks, value_blocks, preferred_element_type=jnp.float32
    )
    own_state = jnp.sum(block_states, 0)
    prefix = prefix_2(own_state, "seq", add_states, jnp.zeros_like(own_state))
    earlier = prefix[None] + jnp.cumsum(block_states, 0) - block_states
    causal = jnp.arange(BLOCK)[:, None] >= jnp.arange(BLOCK)[None, :]

    def one_block(inputs):
        query_rows, key_rows, value_rows, carried = inputs
        scores = jnp.einsum(
            "thd,shd->hts", query_rows, key_rows, preferred_element_type=jnp.float32
        )
        scores = jnp.where(causal[None], scores, 0.0).astype(jnp.bfloat16)
        attended = jnp.einsum(
            "hts,shd->thd", scores, value_rows, preferred_element_type=jnp.float32
        )
        attended = attended + jnp.einsum(
            "thd,hde->the",
            query_rows,
            carried.astype(jnp.bfloat16),
            preferred_element_type=jnp.float32,
        )
        normed = attended * lax.rsqrt(jnp.mean(attended * attended, -1, keepdims=True) + 1e-06)
        return normed.astype(jnp.bfloat16).reshape(BLOCK, local_heads * HD)

    mixed_heads = lax.map(one_block, (query_blocks, key_blocks, value_blocks, earlier)).reshape(
        tok_rows, local_heads * HD
    )
    output = jnp.dot(
        lax.all_gather(mixed_heads, "head", axis=1, tiled=True),
        out_weight,
        preferred_element_type=jnp.float32,
    )
    return output.astype(jnp.bfloat16)


def solution(mesh):
    return jax.shard_map(
        per_device,
        mesh=mesh,
        in_specs=(P("seq", "head"), P("seq", "head"), P("seq", "head"), P(None, "head")),
        out_specs=P("seq", "head"),
        check_vma=False,
    )
```

profile of v0, /device:TPU:1, one launch (start us, length us, event | category | flops | bytes accessed | tf_op | source)
XLA Modules:
  0.0 229.1 jit_solution(4268179932716911457)
XLA Ops:
  6.5 1.4 copy.16
  8.0 2.2 fusion.8
  10.6 5.0 %fusion.6 = f32[1024,2,128]{0,2,1:T(8,128)} fusion(pred[1024,1024]{1,0:T(8,128)(4,1)S(1)} %iota_compare_fusion, bf16[1024,2,128]{0,2,1:T(8,128)(2,1)} %bitcast.47, bf16[1024,256]{1,0:T(8,128)(2,1)} %param.8, bf16[1024,256]{1,0:T(8,128)(2,1)} %param.6), kind=kOutput, calls=%fused_computation.9 | convolution fusion | flops 1077936128 | bytes 3670016 | tf_op jit(solution)/shard_map/while/body/eval_jaxpr/hts,shd->thd/dot_general | solution.py:48
  15.6 62.0 %all-gather.6.cloned.1.call-done = f32[64,128,128]{2,1,0:T(8,128)} async-done(((f32[2,128,128]{2,1,0:T(8,128)}), f32[64,128,128]{2,1,0:T(8,128)}) %all-gather.6.cloned.1.call-update) | async-done | bytes 4194320 | tf_op jit(solution)/shard_map/all_gather | solution.py:12
  77.6 30.1 %while.18 = (s32[]{:T(128)}, f32[2,128,128]{2,1,0:T(8,128)S(1)}, s32[]{:T(128)}, f32[32,2,128,128]{3,2,1,0:T(8,128)}, s32[]{:T(128)}, /*index=5*/s32[]{:T(128)}) while((s32[]{:T(128)}, f32[2,128,128]{2,1,0:T(8,128)S(1)}, s32[]{:T(128)}, f32[32,2,128,128]{3,2,1,0:T(8,128)}, s32[]{:T(128)}, /*index=5*/s32[]{:T(128)}) %tuple.42), condition=%wide.region_1.2_spmd.clone, body=%wide.region_0.0_spmd.clone.sunk | while | flops 98308 | bytes 393317 | solution.py:19
  78.6 0.9 add_select_fusion.2
  79.6 0.9 add_select_fusion.2
  80.5 0.9 add_select_fusion.2
  81.5 0.9 add_select_fusion.2
  82.5 0.9 add_select_fusion.2
  83.5 0.9 add_select_fusion.2
  84.4 0.9 add_select_fusion.2
  85.4 0.9 add_select_fusion.2
  86.4 0.9 add_select_fusion.2
  87.4 0.9 add_select_fusion.2
  88.3 0.9 add_select_fusion.2
  89.3 0.9 add_select_fusion.2
  90.3 0.9 add_select_fusion.2
  91.3 0.9 add_select_fusion.2
  92.2 0.9 add_select_fusion.2
  93.2 0.9 add_select_fusion.2
  94.2 0.9 add_select_fusion.2
  95.1 0.9 add_select_fusion.2
  96.1 0.9 add_select_fusion.2
  97.1 0.9 add_select_fusion.2
  98.1 0.9 add_select_fusion.2
  99.0 0.9 add_select_fusion.2
  100.0 0.9 add_select_fusion.2
  101.0 0.9 add_select_fusion.2
  107.8 1.7 multiply_reduce_fusion
  110.5 105.2 %all-gather.4.cloned.1.call-done = bf16[1024,4096]{0,1:T(8,128)(2,1)} async-done(((bf16[1024,256]{0,1:T(8,128)(2,1)}), bf16[1024,4096]{0,1:T(8,128)(2,1)}) %all-gather.4.cloned.1.call-update) | async-done | bytes 8388624 | tf_op jit(solution)/shard_map/all_gather | solution.py:64
  215.7 6.6 %convolution_convert_fusion = bf16[1024,256]{1,0:T(8,128)(2,1)} fusion(bf16[1024,4096]{0,1:T(8,128)(2,1)} %all-gather.4.cloned.1.call-done, bf16[4096,256]{1,0:T(8,128)(2,1)S(1)} %copy-done), kind=kOutput, calls=%fused_computation.10 | convolution fusion | flops 2147745792 | bytes 11010048 | tf_op jit(solution)/shard_map/dot_general | solution.py:63
  (21 shorter events, 8.0 us)
Async XLA Ops:
  6.5 209.1 %copy-start = (bf16[4096,256]{1,0:T(8,128)(2,1)S(1)}, bf16[4096,256]{1,0:T(8,128)(2,1)}, u32[]{:S(2)}) copy-start(bf16[4096,256]{1,0:T(8,128)(2,1)} %param.9) | copy-start | bytes 6291460
  6.5 71.1 %all-gather.6.cloned.1.call-start = ((), (), s32[]{:S(2)}) async-start(), calls=%async_computation.1 | async-start | bytes 4325376 | tf_op jit(solution)/shard_map/all_gather | solution.py:12
  7.9 2.3 copy-start.2
  10.2 205.5 %all-gather.4.cloned.1.call-start = ((), (), s32[]{:S(2)}) async-start(), calls=%async_computation | async-start | bytes 8912896 | tf_op jit(solution)/shard_map/all_gather | solution.py:64
  10.6 97.2 %copy-start.1 = (f32[2,128,128]{2,1,0:T(8,128)S(1)}, f32[2,128,128]{2,1,0:T(8,128)}, u32[]{:S(2)}) copy-start(f32[2,128,128]{2,1,0:T(8,128)} %fusion.8) | copy-start | bytes 393220
Sparse Core Ops, SparseCore 0:
  10.5 67.0 all-gather.5
  110.6 105.0 all-gather.3
where the time goes:
time: 230 us; the launch traced here: 229 us
  waiting for transfers between devices  167 us (73%)
  other arithmetic  30.7 us (13%)
  matrix products  15.6 us (7%)
  between operations  13.5 us (6%)
    all_gather x1, waiting for transfers between devices, per_device(): lax.all_gather(mixed_heads, 'head', axis=1, tiled=True)  105 us
    all_gather x1, waiting for transfers between devices, prefix_2(): pieces = lax.all_gather(value, axis)  62 us
    select_n x31, other arithmetic, step(): return jnp.where(position < mine, longer, running)  29.4 us
    dot_general x1, matrix products, per_device(): jnp.dot(lax.all_gather(mixed_heads, 'head', axis=1, tiled=True), out_weig...  6.55 us
    dot_general x1, matrix products, one_block(): jnp.einsum('hts,shd->thd', scores, value_rows, preferred_element_type=jnp...  5.05 us
  transfers between devices with their start and end apart: 2, of which 2 were waited for; matrix products, arithmetic and copies ran while one was open for 2% of the time, Pallas kernels for 0%

commit v1 on v0

--- a/solution.py
+++ b/solution.py
@@ -61,7 +61,9 @@
         tok_rows, local_heads * HD
     )
     output = jnp.dot(
-        lax.all_gather(mixed_heads, "head", axis=1, tiled=True),
+        jnp.concatenate(
+            lax.all_to_all(jnp.stack([mixed_heads] * lax.axis_size("head")), "head", 0, 0), axis=1
+        ),
         out_weight,
         preferred_element_type=jnp.float32,
     )

time: 230 us -> 499 us (2.17); the launches traced: 229 us -> 492 us
  blocking collectives: 0 us -> 372 us
  waiting for transfers between devices: 167 us -> 62.1 us
    all_to_all x0 -> x1, blocking collectives: none -> 372 us  [per_device(): lax.all_to_all(jnp.stack([mixed_heads] * lax.axis_size('head')), 'head',...]
    all_gather x1 -> x0, waiting for transfers between devices: 105 us -> none  [per_device(): lax.all_gather(mixed_heads, 'head', axis=1, tiled=True)]
  transfers between devices with their start and end apart: 2 -> 1, of which waited for: 2 -> 1; matrix products, arithmetic and copies ran while one was open for 2% -> 1% of each run, Pallas kernels for 0% -> 0%
where the time goes in v1:
time: 499 us; the launch traced here: 492 us
  blocking collectives  372 us (75%)
  waiting for transfers between devices  62.1 us (12%)
  other arithmetic  29.9 us (6%)
  between operations  13.5 us (3%)
  matrix products  12.2 us (2%)
    all_to_all x1, blocking collectives, per_device(): lax.all_to_all(jnp.stack([mixed_heads] * lax.axis_size('head')), 'head',...  372 us
    all_gather x1, waiting for transfers between devices, prefix_2(): pieces = lax.all_gather(value, axis)  62.1 us
    select_n x31, other arithmetic, step(): return jnp.where(position < mine, longer, running)  29.4 us
  transfers between devices with their start and end apart: 1, of which 1 were waited for; matrix products, arithmetic and copies ran while one was open for 1% of the time, Pallas kernels for 0%

profile of v1, /device:TPU:1, one launch (start us, length us, event | category | flops | bytes accessed | tf_op | source)
XLA Modules:
  0.0 492.3 jit_solution(12565084924182406021)
XLA Ops:
  6.5 1.4 copy.24
  8.0 2.2 fusion.8
  10.5 5.1 %fusion.6 = f32[1024,2,128]{0,2,1:T(8,128)} fusion(pred[1024,1024]{1,0:T(8,128)(4,1)S(1)} %iota_compare_fusion, bf16[1024,2,128]{0,2,1:T(8,128)(2,1)} %bitcast.51, bf16[1024,256]{1,0:T(8,128)(2,1)} %param.8, bf16[1024,256]{1,0:T(8,128)(2,1)} %param.6), kind=kOutput, calls=%fused_computation.9 | convolution fusion | flops 1077936128 | bytes 3670016 | tf_op jit(solution)/shard_map/while/body/eval_jaxpr/hts,shd->thd/dot_general | solution.py:48
  15.6 62.1 %all-gather.3.cloned.1.call-done = f32[64,128,128]{2,1,0:T(8,128)} async-done(((f32[2,128,128]{2,1,0:T(8,128)}), f32[64,128,128]{2,1,0:T(8,128)}) %all-gather.3.cloned.1.call-update) | async-done | bytes 4194320 | tf_op jit(solution)/shard_map/all_gather | solution.py:12
  77.6 30.1 %while.18 = (s32[]{:T(128)}, f32[2,128,128]{2,1,0:T(8,128)S(1)}, s32[]{:T(128)}, f32[32,2,128,128]{3,2,1,0:T(8,128)}, s32[]{:T(128)}, /*index=5*/s32[]{:T(128)}) while((s32[]{:T(128)}, f32[2,128,128]{2,1,0:T(8,128)S(1)}, s32[]{:T(128)}, f32[32,2,128,128]{3,2,1,0:T(8,128)}, s32[]{:T(128)}, /*index=5*/s32[]{:T(128)}) %tuple.40), condition=%wide.region_1.2_spmd.clone, body=%wide.region_0.0_spmd.clone.sunk | while | flops 98308 | bytes 393317 | solution.py:19
  78.6 0.9 add_select_fusion.2
  79.6 0.9 add_select_fusion.2
  80.5 0.9 add_select_fusion.2
  81.5 0.9 add_select_fusion.2
  82.5 0.9 add_select_fusion.2
  83.5 0.9 add_select_fusion.2
  84.4 0.9 add_select_fusion.2
  85.4 0.9 add_select_fusion.2
  86.4 0.9 add_select_fusion.2
  87.4 0.9 add_select_fusion.2
  88.3 0.9 add_select_fusion.2
  89.3 0.9 add_select_fusion.2
  90.3 0.9 add_select_fusion.2
  91.3 0.9 add_select_fusion.2
  92.2 0.9 add_select_fusion.2
  93.2 0.9 add_select_fusion.2
  94.2 0.9 add_select_fusion.2
  95.1 0.9 add_select_fusion.2
  96.1 0.9 add_select_fusion.2
  97.1 0.9 add_select_fusion.2
  98.1 0.9 add_select_fusion.2
  99.0 0.9 add_select_fusion.2
  100.0 0.9 add_select_fusion.2
  107.8 1.7 multiply_reduce_fusion
  109.7 1.1 stack.3
  110.7 371.5 %all_to_all.5 = bf16[16,1024,256]{1,2,0:T(8,128)(2,1)S(1)} all-to-all(bf16[16,1024,256]{1,2,0:T(8,128)(2,1)S(1)} %stack.3), channel_id=1, replica_groups=mesh['seq'=32,'head'=16] {'head'}, dimensions={0} | all-to-all | bytes 16777216 | tf_op jit(solution)/shard_map/all_to_all | solution.py:65
  482.3 3.2 convolution_convert_fusion
  (20 shorter events, 8.1 us)
Async XLA Ops:
  6.5 475.7 %copy-start = (bf16[4096,256]{1,0:T(8,128)(2,1)S(1)}, bf16[4096,256]{1,0:T(8,128)(2,1)}, u32[]{:S(2)}) copy-start(bf16[4096,256]{1,0:T(8,128)(2,1)} %param.9) | copy-start | bytes 6291460
  6.5 71.1 %all-gather.3.cloned.1.call-start = ((), (), s32[]{:S(2)}) async-start(), calls=%async_computation.1 | async-start | bytes 4325376 | tf_op jit(solution)/shard_map/all_gather | solution.py:12
  7.9 2.2 copy-start.2
  10.5 97.3 %copy-start.1 = (f32[2,128,128]{2,1,0:T(8,128)S(1)}, f32[2,128,128]{2,1,0:T(8,128)}, u32[]{:S(2)}) copy-start(f32[2,128,128]{2,1,0:T(8,128)} %fusion.8) | copy-start | bytes 393220
Sparse Core Ops, SparseCore 0:
  10.5 67.0 all-gather.2
